TPU v7x, 32 devices: a whole 2x2x4 slice. The times are simulated.
32 devices in a mesh: dp: 2 (over y), row: 4 (over x, core), col: 4 (over z).
Axes of the slice: x: 2, y: 2, z: 4, core: 2. Of those that a mesh axis runs over, the one named last changes fastest.
Arguments:
- grad_out: bfloat16 [512, 8192], P(('dp', 'col'), 'row'), may hold values from -6 to 6
- saved_hidden: bfloat16 [512, 26624], P(('dp', 'row'), 'col'), may hold values from -0.26367188 to 0.26367188
- down_weight: bfloat16 [26624, 8192], P('col', 'row'), may hold values from -0.0625 to 0.0625
Outputs:
- input_grad: bfloat16 [512, 26624], P(('dp', 'row'), 'col')
- weight_grad: bfloat16 [26624, 8192], P(('col', 'dp'), 'row')
All inputs are finite; a program needn't handle non-finite values.
Results may differ from a plain program's by a relative error of at most 0.001.
Values may be sent and summed in bfloat16 or wider, within the bound.
No kernel may reach another device: no remote copies, remote signals or barrier semaphores. Data moves between devices by JAX's collectives and lax.ppermute only.
A program may use at most 128 MiB of HBM per device.

v0:
```python
import jax
import jax.numpy as jnp
from jax import lax
from jax.sharding import PartitionSpec as P


def local(grad_out, saved_hidden, down_weight):
    local_rows = saved_hidden.shape[0]
    gathered_all = lax.all_gather(grad_out, ("dp", "col"), axis=0, tiled=True)
    copy_count = lax.axis_size("dp")
    row_count = lax.axis_size("row")
    copy_rows = gathered_all.shape[0] // copy_count
    grad_copy = lax.dynamic_slice_in_dim(
        gathered_all, lax.axis_index("dp") * copy_rows, copy_rows, 0
    )
    hidden_parts = lax.all_to_all(saved_hidden, "dp", split_axis=1, concat_axis=0, tiled=True)
    hidden_stack = lax.all_gather(hidden_parts, "row", axis=0, tiled=True)
    hidden_grid = hidden_stack.reshape(row_count, copy_count, local_rows, hidden_stack.shape[1])
    grad_grid = gathered_all.reshape(copy_count, row_count, local_rows, gathered_all.shape[1])
    weight_grad = jnp.einsum(
        "rdtk,drtn->kn", hidden_grid, grad_grid, preferred_element_type=jnp.float32
    )
    input_grad = lax.psum_scatter(
        lax.dot_general(
            grad_copy, down_weight, (((1,), (1,)), ((), ())), preferred_element_type=jnp.float32
        ),
        "row",
        scatter_dimension=0,
        tiled=True,
    )
    return (input_grad.astype(jnp.bfloat16), weight_grad.astype(jnp.bfloat16))


def solution(mesh):
    placed = (P(("dp", "col"), "row"), P(("dp", "row"), "col"), P("col", "row"))
    return jax.shard_map(
        local,
        mesh=mesh,
        in_specs=placed,
        out_specs=(P(("dp", "row"), "col"), P(("col", "dp"), "row")),
        check_vma=False,
    )
```

profile of v0, /device:TPU:0, one launch (start us, length us, event | category | flops | bytes accessed | tf_op | source)
XLA Modules:
  0.0 167.5 jit_solution(16563208441328073580)
XLA Ops:
  7.2 0.0 all-gather.3.cloned.1.call-start
  7.2 0.7 all-gather.3.cloned.1.call-update
  7.9 0.0 all-gather.5.cloned.1.call-start
  7.9 1.2 copy.15
  9.2 18.8 %all_to_all.19 = bf16[64,2,3328]{2,0,1:T(8,128)(2,1)} all-to-all(bf16[64,2,3328]{2,0,1:T(8,128)(2,1)S(1)} %bitcast.16), channel_id=1, replica_groups=mesh['dp'=2,'row'=4,'col'=4] {'dp'}, dimensions={1} | all-to-all | bytes 1703936 | tf_op jit(solution)/shard_map/all_to_all | solution.py:16
  28.0 0.0 all-gather.5.cloned.1.call-update
  28.0 0.0 reduce-scatter.2.cloned.1.call-start
  28.1 35.4 %all-gather.3.cloned.1.call-done = bf16[512,2048]{1,0:T(8,128)(2,1)} async-done(((bf16[64,2048]{1,0:T(8,128)(2,1)}), bf16[512,2048]{1,0:T(8,128)(2,1)}) %all-gather.3.cloned.1.call-update) | async-done | bytes 2097168 | tf_op jit(solution)/shard_map/all_gather | solution.py:9
  63.5 16.8 %fusion.1 = f32[256,6656]{1,0:T(8,128)} fusion(bf16[6656,2048]{1,0:T(8,128)(2,1)} %param.5, bf16[512,2048]{1,0:T(8,128)(2,1)} %all-gather.3.cloned.1.call-done, s32[]{:T(128)S(6)} %select_n.3), kind=kOutput, calls=%fused_computation.2 | convolution fusion | flops 6979321856 | bytes 35127300 | tf_op jit(solution)/shard_map/dot_general | solution.py:24
  80.2 0.0 copy-start
  80.2 0.0 reduce-scatter.2.cloned.1.call-update
  80.3 13.3 %all-gather.5.cloned.1.call-done = bf16[512,3328]{1,0:T(8,128)(2,1)} async-done(((bf16[128,3328]{1,0:T(8,128)(2,1)}), bf16[512,3328]{1,0:T(8,128)(2,1)}) %all-gather.5.cloned.1.call-update) | async-done | bytes 3407888 | tf_op jit(solution)/shard_map/all_gather | solution.py:17
  93.6 0.0 copy-done
  93.6 13.3 %bitcast_convert_fusion = bf16[3328,2048]{1,0:T(8,128)(2,1)} fusion(bf16[2,4,64,2048]{3,2,1,0:T(8,128)(2,1)S(1)} %bitcast.19, bf16[4,2,64,3328]{3,2,1,0:T(8,128)(2,1)} %bitcast.18), kind=kOutput, calls=%fused_computation | convolution fusion | flops 6986137600 | bytes 19136512 | tf_op jit(solution)/shard_map/rdtk,drtn->kn/dot_general | solution.py:20
  106.9 51.6 %reduce-scatter.2.cloned.1.call-done = f32[64,6656]{1,0:T(8,128)} async-done(((f32[256,6656]{1,0:T(8,128)}), f32[64,6656]{1,0:T(8,128)}) %reduce-scatter.2.cloned.1.call-update) | async-done | bytes 1703952 | tf_op jit(solution)/shard_map/reduce_scatter | solution.py:23
  158.6 2.4 %convert_element_type.6 = bf16[64,6656]{1,0:T(8,128)(2,1)} convert(f32[64,6656]{1,0:T(8,128)} %reduce-scatter.2.cloned.1.call-done) | non-fusion elementwise | flops 425984 | bytes 2555904 | tf_op jit(solution)/shard_map/convert_element_type | solution.py:31
Async XLA Ops:
  7.2 56.3 %all-gather.3.cloned.1.call-start = ((), (), s32[]{:S(2)}) async-start(), calls=%async_computation.2 | async-start | bytes 2359296 | tf_op jit(solution)/shard_map/all_gather | solution.py:9
  7.9 85.7 %all-gather.5.cloned.1.call-start = ((), (), s32[]{:S(2)}) async-start(), calls=%async_computation.4 | async-start | bytes 4259840 | tf_op jit(solution)/shard_map/all_gather | solution.py:17
  28.0 130.6 %reduce-scatter.2.cloned.1.call-start = ((), (), s32[]{:S(2)}) async-start(), calls=%async_computation.3 | async-start | bytes 8519680 | tf_op jit(solution)/shard_map/reduce_scatter | solution.py:23
  80.2 13.4 %copy-start = (bf16[512,2048]{1,0:T(8,128)(2,1)S(1)}, bf16[512,2048]{1,0:T(8,128)(2,1)}, u32[]{:S(2)}) copy-start(bf16[512,2048]{1,0:T(8,128)(2,1)} %all-gather.3.cloned.1.call-done) | copy-start | bytes 6291460
Sparse Core Ops, SparseCore 0:
  10.1 53.3 all-gather.2
  65.0 28.5 all-gather.4
  96.1 62.3 reduce-scatter.1
where the time goes:
time: 168 us
  waiting for transfers between devices  101 us (60%)
  matrix products  30.1 us (18%)
  blocking collectives  18.8 us (11%)
  between operations  13.8 us (8%)
  other arithmetic  2.44 us (1%)
    reduce_scatter x1, waiting for transfers between devices, local(): lax.psum_scatter(lax.dot_general(grad_copy, down_weight, (((1,), (1,)), (...  51.6 us
    all_gather x1, waiting for transfers between devices, local(): gathered_all = lax.all_gather(grad_out, ('dp', 'col'), axis=0, tiled=True)  35.4 us
    all_to_all x1, blocking collectives, local(): lax.all_to_all(saved_hidden, 'dp', split_axis=1, concat_axis=0, tiled=True)  18.8 us
    dot_general x1, matrix products, local(): lax.dot_general(grad_copy, down_weight, (((1,), (1,)), ((), ())), preferr...  16.8 us
    all_gather x1, waiting for transfers between devices, local(): hidden_stack = lax.all_gather(hidden_parts, 'row', axis=0, tiled=True)  13.3 us
    dot_general x1, matrix products, local(): jnp.einsum('rdtk,drtn->kn', hidden_grid, grad_grid, preferred_element_typ...  13.3 us
  transfers between devices with their start and end apart: 3, of which 3 were waited for; matrix products, arithmetic and copies ran while one was open for 19% of the time, Pallas kernels for 0%

commit v1 on v0

--- a/solution.py
+++ b/solution.py
@@ -1,10 +1,27 @@
+import functools
+
 import jax
 import jax.numpy as jnp
 from jax import lax
+from jax.experimental import pallas as pl
+from jax.experimental.pallas import tpu as pltpu
 from jax.sharding import PartitionSpec as P
 
 
-def local(grad_out, saved_hidden, down_weight):
+CORES = 2
+CHUNKS = 4
+NT = (((1,), (1,)), ((), ()))
+TN = (((0,), (0,)), ((), ()))
+SMALL = 12 * 2**20
+SPLIT = 4
+WIDE_LIMIT = 36 * 2**20
+GRAD_MOST = 6.0
+WEIGHT_MOST = 0.0625
+POWER = 8
+TOP = 120.0
+
+
+def native(grad_out, saved_hidden, down_weight):
     local_rows = saved_hidden.shape[0]
     gathered_all = lax.all_gather(grad_out, ("dp", "col"), axis=0, tiled=True)
     copy_count = lax.axis_size("dp")
@@ -29,6 +46,321 @@
         tiled=True,
     )
     return (input_grad.astype(jnp.bfloat16), weight_grad.astype(jnp.bfloat16))
+
+
+def encode(value, scale):
+    scaled = value * scale
+    square = scaled * scaled
+    fourth = square * square
+    eighth = fourth * fourth
+    return jnp.where(scaled < 0, -eighth, eighth).astype(jnp.bfloat16)
+
+
+def decode(code, scale):
+    wide = code.astype(jnp.float32)
+    half = lax.rsqrt(jnp.maximum(jnp.abs(wide), 2.0**-126))
+    fourth = lax.rsqrt(half)
+    root = fourth * lax.rsqrt(fourth) * (1.0 / scale)
+    return jnp.where(wide < 0, -root, jnp.where(wide > 0, root, 0.0))
+
+
+def swap(x, axis, mask):
+    n = lax.axis_size(axis)
+    return lax.ppermute(x, axis, [(i, i ^ mask) for i in range(n)])
+
+
+def put_blocks(at, blocks, held):
+    rows = blocks[0].shape[0]
+    for i, block in enumerate(blocks):
+        held[pl.ds(pl.multiple_of(at[i] * rows, rows), rows), :] = block[...]
+
+
+def load_kernel(corners, w, *refs):
+    outs, sem = refs[:-1], refs[-1]
+    copies = []
+    for (lo, side), out in zip(corners, outs):
+        tall, half = out.shape
+        step = tall // SPLIT
+        for i in range(SPLIT):
+            part = w.at[pl.ds(lo + i * step, step), pl.ds(side * half, half)]
+            copies.append(pltpu.make_async_copy(part, out.at[pl.ds(i * step, step)], sem.at[len(copies)]))
+    for c in copies:
+        c.start()
+    return copies
+
+
+def load_only(corners, w, *refs):
+    for c in load_kernel(corners, w, *refs):
+        c.wait()
+
+
+def load(weight, corners, tall):
+    half = weight.shape[1] // 2
+    outs = pl.pallas_call(
+        functools.partial(load_only, corners),
+        in_specs=[pl.BlockSpec(memory_space=pltpu.HBM)],
+        out_specs=[pl.BlockSpec(memory_space=pltpu.VMEM)] * len(corners),
+        out_shape=[pltpu.VMEM((tall, half), weight.dtype)] * len(corners),
+        scratch_shapes=[pltpu.SemaphoreType.DMA((SPLIT * len(corners),))],
+        cost_estimate=pl.CostEstimate(
+            flops=0, bytes_accessed=2 * len(corners) * tall * half, transcendentals=0
+        ),
+        compiler_params=pltpu.CompilerParams(vmem_limit_bytes=SMALL),
+    )(pltpu.with_memory_space_constraint(weight, pltpu.HBM))
+    return outs
+
+
+def first_kernel(n, corners, at, b0, b1, b2, b3, w, *refs):
+    now, acc, later, held, sem = refs[:n], refs[n], refs[n + 1 : -2], refs[-2], refs[-1]
+    copies = load_kernel(corners, w, *later, sem)
+    put_blocks(at, (b0, b1, b2, b3), held)
+    tall = now[0].shape[0]
+    for i, ref in enumerate(now):
+        acc[:, i * tall : (i + 1) * tall] = lax.dot_general(
+            held[...], ref[...], NT, preferred_element_type=jnp.float32
+        )
+    for c in copies:
+        c.wait()
+
+
+def first_half(at, blocks, weight, now, corners):
+    rows = 4 * blocks[0].shape[0]
+    tall, half = now[0].shape
+    whole = pl.BlockSpec(memory_space=pltpu.VMEM)
+    outs = pl.pallas_call(
+        functools.partial(first_kernel, len(now), corners),
+        grid=(1,),
+        in_specs=[pl.BlockSpec(memory_space=pltpu.SMEM)]
+        + [pl.BlockSpec((b.shape[0], half), lambda i: (0, 0)) for b in blocks]
+        + [pl.BlockSpec(memory_space=pltpu.HBM)]
+        + [whole] * len(now),
+        out_specs=[whole] * (1 + len(corners)),
+        out_shape=[pltpu.VMEM((rows, tall * len(now)), jnp.float32)]
+        + [pltpu.VMEM((tall, half), weight.dtype)] * len(corners),
+        scratch_shapes=[
+            pltpu.VMEM((rows, half), weight.dtype),
+            pltpu.SemaphoreType.DMA((SPLIT * len(corners),)),
+        ],
+        cost_estimate=pl.CostEstimate(
+            flops=2 * rows * tall * len(now) * half,
+            bytes_accessed=2 * len(corners) * tall * half,
+            transcendentals=0,
+        ),
+        compiler_params=pltpu.CompilerParams(vmem_limit_bytes=SMALL),
+    )(at, *blocks, pltpu.with_memory_space_constraint(weight, pltpu.HBM), *now)
+    return outs[0], outs[1:]
+
+
+def second_kernel(lo, n_now, corners, at, b0, b1, b2, b3, w, *refs):
+    n = len(corners)
+    now, rest = refs[:n_now], refs[n_now:]
+    acc, rest = (rest[0], rest[1:]) if lo is not None else (None, rest)
+    keep, give, later, held = rest[0], rest[1], rest[2 : 2 + n], rest[2 + n]
+    copies = load_kernel(corners, w, *later, rest[-1]) if n else []
+    put_blocks(at, (b0, b1, b2, b3), held)
+    top, tall = keep.shape
+    half = now[0].shape[1]
+    part = lax.dot_general(
+        held[:, -half:], now[-1][...], NT, preferred_element_type=jnp.float32
+    )
+    if acc is None:
+        part += lax.dot_general(held[:, :half], now[0][...], NT, preferred_element_type=jnp.float32)
+    else:
+        part += acc[:, lo : lo + tall]
+    keep[...] = part[:top]
+    give[...] = part[top:]
+    for c in copies:
+        c.wait()
+
+
+def second_half(at, blocks, weight, now, acc, lo, corners=()):
+    rows = 4 * blocks[0].shape[0]
+    tall, half = now[0].shape
+    wide = half * len(now)
+    whole = pl.BlockSpec(memory_space=pltpu.VMEM)
+    scratch = [pltpu.VMEM((rows, wide), weight.dtype)]
+    if corners:
+        scratch.append(pltpu.SemaphoreType.DMA((SPLIT * len(corners),)))
+    outs = pl.pallas_call(
+        functools.partial(second_kernel, None if acc is None else lo, len(now), corners),
+        grid=(1,),
+        in_specs=[pl.BlockSpec(memory_space=pltpu.SMEM)]
+        + [
+            pl.BlockSpec((b.shape[0], wide), lambda i, at=b.shape[1] // wide - 1: (0, at))
+            for b in blocks
+        ]
+        + [pl.BlockSpec(memory_space=pltpu.HBM)]
+        + [whole] * (len(now) + (acc is not None)),
+        out_specs=[whole] * (2 + len(corners)),
+        out_shape=[jax.ShapeDtypeStruct((rows // 2, tall), jnp.float32)] * 2
+        + [pltpu.VMEM((tall, half), weight.dtype)] * len(corners),
+        scratch_shapes=scratch,
+        cost_estimate=pl.CostEstimate(
+            flops=2 * rows * tall * wide, bytes_accessed=2 * tall * wide, transcendentals=0
+        ),
+        compiler_params=pltpu.CompilerParams(vmem_limit_bytes=SMALL),
+    )(
+        at,
+        *blocks,
+        pltpu.with_memory_space_constraint(weight, pltpu.HBM),
+        *now,
+        *([] if acc is None else [acc]),
+    )
+    return outs[0], outs[1], outs[2:]
+
+
+def finish_kernel(scale, *refs):
+    out = refs[-1]
+    rows = out.shape[0]
+    lo = 0
+    for keep, got, far in zip(refs[0:-1:3], refs[1:-1:3], refs[2:-1:3]):
+        tall = far.shape[1]
+        value = (keep[:rows] + got[:rows]) + decode(far[...], scale)
+        out[:, lo : lo + tall] = value.astype(out.dtype)
+        lo += tall
+
+
+def finish(parts, scale, dtype):
+    rows = parts[0][2].shape[0]
+    whole = pl.BlockSpec(memory_space=pltpu.VMEM)
+    hid = sum(p[2].shape[1] for p in parts)
+    return pl.pallas_call(
+        functools.partial(finish_kernel, scale),
+        in_specs=[whole] * (3 * len(parts)),
+        out_specs=whole,
+        out_shape=jax.ShapeDtypeStruct((rows, hid), dtype),
+        cost_estimate=pl.CostEstimate(
+            flops=20 * rows * hid, bytes_accessed=14 * rows * hid, transcendentals=0
+        ),
+        compiler_params=pltpu.CompilerParams(vmem_limit_bytes=SMALL),
+    )(*[x for p in parts for x in p])
+
+
+def weight_kernel(counts, at, *refs):
+    rows = refs[0].shape[0]
+    n_hid, n_grad = len(counts), sum(counts)
+    hidden, grads, out, held = refs[:n_hid], refs[n_hid : n_hid + n_grad], *refs[-2:]
+    wide = out.shape[1]
+
+    @pl.when((pl.program_id(0) == 0) & (pl.program_id(1) == 0))
+    def _():
+        left = list(grads)
+        for i, count in enumerate(counts):
+            place = at[i % 4] + 4 * (i // 4)
+            lanes = 0
+            for piece in left[:count]:
+                span = piece.shape[1]
+                start = pl.multiple_of(place * rows, rows)
+                held[pl.ds(start, rows), lanes : lanes + span] = piece[...]
+                lanes += span
+            left = left[count:]
+
+    stacked = jnp.concatenate([h[...] for h in hidden])
+    start = pl.multiple_of(pl.program_id(1) * wide, wide)
+    out[...] = lax.dot_general(
+        stacked, held[:, pl.ds(start, wide)], TN, preferred_element_type=jnp.float32
+    ).astype(out.dtype)
+
+
+def weight_product(at, hidden, grads):
+    pieces = [g if isinstance(g, tuple) else (g,) for g in grads]
+    rows, hid = hidden[0].shape
+    depth = sum(p.shape[1] for p in pieces[0])
+    tall, wide = hid // 2, depth // 2
+    tokens = rows * len(hidden)
+    flat = [p for group in pieces for p in group]
+    return pl.pallas_call(
+        functools.partial(weight_kernel, [len(p) for p in pieces]),
+        grid=(hid // tall, depth // wide),
+        in_specs=[pl.BlockSpec(memory_space=pltpu.SMEM)]
+        + [pl.BlockSpec((rows, tall), lambda i, j: (0, i)) for _ in hidden]
+        + [pl.BlockSpec(p.shape, lambda i, j: (0, 0)) for p in flat],
+        out_specs=pl.BlockSpec((tall, wide), lambda i, j: (i, j)),
+        out_shape=jax.ShapeDtypeStruct((hid, depth), hidden[0].dtype),
+        scratch_shapes=[pltpu.VMEM((tokens, depth), hidden[0].dtype)],
+        cost_estimate=pl.CostEstimate(
+            flops=2 * tokens * hid * depth, bytes_accessed=2 * hid * depth, transcendentals=0
+        ),
+        compiler_params=pltpu.CompilerParams(vmem_limit_bytes=WIDE_LIMIT),
+    )(at, *hidden, *flat)
+
+
+def paired(grad_out, saved_hidden, down_weight):
+    d, r, z = (lax.axis_index(a) for a in ("dp", "row", "col"))
+    chip = CORES
+    rows = saved_hidden.shape[0]
+    hid, depth = down_weight.shape
+    half = hid // 2
+    cut = depth // 2
+
+    h_give = lax.dynamic_slice_in_dim(saved_hidden, (1 - d) * half, half, 1)
+    h_peer = swap(h_give, "dp", 1)
+    rev_a = swap(grad_out[:, :cut], "col", 3)
+    pair = swap(grad_out, "col", 1)
+    h_mine = lax.dynamic_slice_in_dim(saved_hidden, d * half, half, 1)
+    h_far = swap(h_mine, "row", chip)
+    rev_b = swap(grad_out[:, cut:], "col", 3)
+    y_own = swap(grad_out, "dp", 1)
+    s2_a = swap(rev_a, "col", 1)
+    s2_b = swap(rev_b, "col", 1)
+    h_peer_far = swap(h_peer, "row", chip)
+    y_pair = swap(pair, "dp", 1)
+    rev = jnp.concatenate([rev_a, rev_b], 1)
+    s2 = jnp.concatenate([s2_a, s2_b], 1)
+    y_rev = swap(rev, "dp", 1)
+    y_s2 = swap(y_rev, "col", 1)
+    mine = [h_mine, h_peer, h_far, h_peer_far]
+    mate = [swap(h, "row", 1) for h in mine]
+
+    ks = [r ^ z ^ m for m in (0, 1, 3, 2)]
+    at = jnp.stack([((k & 1) << 1) | (k >> 1) for k in ks]).astype(jnp.int32)
+    scale = 2.0 ** (TOP / POWER) / (CORES * depth * GRAD_MOST * WEIGHT_MOST)
+    tall = hid // CHUNKS
+    spots = [i * tall for i in range(CHUNKS)]
+    early = CHUNKS - 1
+    held = {}
+
+    def fetch(keys, outs):
+        held.update(zip(keys, outs))
+
+    plan = [(i, s) for s in range(2) for i in range(early)]
+    groups = [plan[:2], plan[2:4], plan[4:]]
+    at_corner = [[(spots[i], s) for i, s in g] for g in groups]
+    for n in range(2):
+        fetch(groups[n], load(down_weight, at_corner[n], tall))
+    now = [held[i, 0] for i in range(early)]
+    acc, outs = first_half(at, (grad_out, pair, rev_a, s2_a), down_weight, now, at_corner[2])
+    fetch(groups[2], outs)
+    parts = []
+    for i, lo in enumerate(spots):
+        if i < early:
+            keys = [(early, i - 1)] if i else []
+            corners = [(spots[early], s) for _, s in keys]
+            blocks = (grad_out, pair, rev_b, s2_b)
+            keep, give, outs = second_half(at, blocks, down_weight, [held[i, 1]], acc, lo, corners)
+            fetch(keys, outs)
+        else:
+            blocks = (grad_out, pair, rev, s2)
+            now = [held[early, s] for s in range(2)]
+            keep, give, _ = second_half(at, blocks, down_weight, now, None, lo)
+        got = swap(give, "row", 1)
+        sent = encode(keep[rows:] + got[rows:], scale)
+        parts.append((keep, got, swap(sent, "row", chip)))
+    input_grad = finish(parts, scale, saved_hidden.dtype)
+
+    weight_grad = weight_product(
+        at,
+        [mine[0], mine[2], mate[0], mate[2], mine[1], mine[3], mate[1], mate[3]],
+        [grad_out, pair, rev, s2, y_own, y_pair, y_rev, y_s2],
+    )
+    return input_grad, weight_grad
+
+
+def local(grad_out, saved_hidden, down_weight):
+    sizes = [lax.axis_size(a) for a in ("dp", "row", "col")]
+    if sizes[0] == 2 and sizes[1] == 2 * CORES and sizes[2] == sizes[1]:
+        return paired(grad_out, saved_hidden, down_weight)
+    return native(grad_out, saved_hidden, down_weight)
 
 
 def solution(mesh):

time: 168 us -> 93.4 us (0.56)
  waiting for transfers between devices: 101 us -> 19.9 us
  Pallas kernels: 0 us -> 36.3 us
  matrix products: 30.1 us -> 0 us
  starting transfers between devices: 0.12 us -> 24.2 us
  blocking collectives: 18.8 us -> 0 us
  between operations: 13.8 us -> 0.87 us
  local copies, waits for them, and re-layouts: 1.22 us -> 10.2 us
    reduce_scatter x1 -> x0, waiting for transfers between devices: 51.6 us -> none  [local(): lax.psum_scatter(lax.dot_general(grad_copy, down_weight, (((1,), (1,)), (...]
    all_gather x2 -> x0, waiting for transfers between devices: 48.7 us -> none  [the longest x1 35.4 us: local(): gathered_all = lax.all_gather(grad_out, ('dp', 'col'), axis=0, tiled=True)]
    pallas_call x0 -> x9, Pallas kernels: none -> 36.3 us  [the longest x4 11.5 us: second_half(): pl.pallas_call(functools.partial(second_kernel, None if acc is None else...]
    dot_general x2 -> x0, matrix products: 30.1 us -> none  [the longest x1 16.8 us: local(): lax.dot_general(grad_copy, down_weight, (((1,), (1,)), ((), ())), preferr...]
    ppermute x0 -> x24, starting transfers between devices: none -> 24.2 us  [swap(): return lax.ppermute(x, axis, [(i, i ^ mask) for i in range(n)])]
    ppermute x0 -> x24, waiting for transfers between devices: none -> 19.9 us  [swap(): return lax.ppermute(x, axis, [(i, i ^ mask) for i in range(n)])]
    all_to_all x1 -> x0, blocking collectives: 18.8 us -> none  [local(): lax.all_to_all(saved_hidden, 'dp', split_axis=1, concat_axis=0, tiled=True)]
    unnamed x2 -> x26, local copies, waits for them, and re-layouts: 0.01 us -> 7.99 us
  transfers between devices with their start and end apart: 3 -> 24, of which waited for: 3 -> 9; matrix products, arithmetic and copies ran while one was open for 19% -> 3% of each run, Pallas kernels for 0% -> 25%
where the time goes in v1:
time: 93.4 us; the launch traced here: 93 us
  Pallas kernels  36.3 us (39%)
  starting transfers between devices  24.2 us (26%)
  waiting for transfers between devices  19.9 us (21%)
  local copies, waits for them, and re-layouts  10.2 us (11%)
  other arithmetic  1.59 us (2%)
    ppermute x24, starting transfers between devices, swap(): return lax.ppermute(x, axis, [(i, i ^ mask) for i in range(n)])  24.2 us
    ppermute x24, waiting for transfers between devices, swap(): return lax.ppermute(x, axis, [(i, i ^ mask) for i in range(n)])  19.9 us
    pallas_call x4, Pallas kernels, second_half(): pl.pallas_call(functools.partial(second_kernel, None if acc is None else...  11.5 us
    pallas_call x1, Pallas kernels, weight_product(): pl.pallas_call(functools.partial(weight_kernel, [len(p) for p in pieces])...  11.4 us
    unnamed x26, local copies, waits for them, and re-layouts  7.99 us
    pallas_call x2, Pallas kernels, load(): pl.pallas_call(functools.partial(load_only, corners), in_specs=[pl.BlockS...  6.1 us
    pallas_call x1, Pallas kernels, first_half(): pl.pallas_call(functools.partial(first_kernel, len(now), corners), grid=(...  4.34 us
    pallas_call x1, Pallas kernels, finish(): pl.pallas_call(functools.partial(finish_kernel, scale), in_specs=[whole]...  2.93 us
  transfers between devices with their start and end apart: 24, of which 9 were waited for; matrix products, arithmetic and copies ran while one was open for 3% of the time, Pallas kernels for 25%

profile of v1, /device:TPU:0, one launch (start us, length us, event | category | flops | bytes accessed | tf_op | source)
XLA Modules:
  0.0 93.0 jit_solution(8688170729747126140)
XLA Ops:
  0.6 1.0 %fusion.8 = (bf16[64,1024]{1,0:T(8,128)(2,1)S(1)}, bf16[64,1024]{1,0:T(8,128)(2,1)S(1)}) fusion(bf16[64,2048]{1,0:T(8,128)(2,1)} %refs_8_.1), kind=kLoop, calls=%fused_computation.23 | loop fusion | bytes 524288 | tf_op jit(solution)/shard_map/slice | solution.py:298
  1.6 5.1 %collective-permute-start.3 = (bf16[64,1024]{1,0:T(8,128)(2,1)S(1)}, bf16[64,1024]{1,0:T(8,128)(2,1)S(1)}, u32[]{:S(2)}, u32[]{:S(2)}) collective-permute-start(bf16[64,1024]{1,0:T(8,128)(2,1)S(1)} %get-tuple-element.38), channel_id=1, source_target_pairs={{0,3},{1,2},{2,1},{3,0},{4,7},{5,6},{6,5},{7,4},{8,11},{9,10},{10,... | collective-permute-start | bytes 393224 | tf_op jit(solution)/shard_map/ppermute | solution.py:69
  7.7 3.0 %shard_map.51 = (bf16[1664,1024]{1,0:T(8,128)(2,1)S(1)}, bf16[1664,1024]{1,0:T(8,128)(2,1)S(1)}) custom-call(bf16[6656,2048]{1,0:T(8,128)(2,1)} %w.13), custom_call_target="tpu_custom_call" | custom-call | bytes 6815744 | tf_op jit(solution)/shard_map/pallas_call | solution.py:99
  10.8 3.1 %shard_map.50 = (bf16[1664,1024]{1,0:T(8,128)(2,1)S(1)}, bf16[1664,1024]{1,0:T(8,128)(2,1)S(1)}) custom-call(bf16[6656,2048]{1,0:T(8,128)(2,1)} %w.13), custom_call_target="tpu_custom_call" | custom-call | bytes 6815744 | tf_op jit(solution)/shard_map/pallas_call | solution.py:99
  13.9 1.7 %copy-done.3 = bf16[1664,1024]{1,0:T(8,128)(2,1)} copy-done((bf16[1664,1024]{1,0:T(8,128)(2,1)}, bf16[1664,1024]{1,0:T(8,128)(2,1)S(1)}, u32[]{:S(2)}) %copy-start.3) | copy-done | bytes 3407896
  15.6 1.1 %collective-permute-start.4 = (bf16[64,1024]{1,0:T(8,128)(2,1)S(1)}, bf16[64,1024]{1,0:T(8,128)(2,1)S(1)}, u32[]{:S(2)}, u32[]{:S(2)}) collective-permute-start(bf16[64,1024]{1,0:T(8,128)(2,1)S(1)} %collective-permute-done.3.b2), channel_id=1, source_target_pairs={{0,1},{1,0},{2,3},{3,2},{4,5},{5,4},{6,7},{7,6},{8,9},{9,8},{10,11... | collective-permute-start | bytes 393224 | tf_op jit(solution)/shard_map/ppermute | solution.py:69
  16.7 2.4 %collective-permute-done.1.b2 = bf16[64,1024]{1,0:T(8,128)(2,1)S(1)} collective-permute-done((bf16[64,1024]{1,0:T(8,128)(2,1)S(1)}, bf16[64,1024]{1,0:T(8,128)(2,1)S(1)}, u32[]{:S(2)}, u32[]{:S(2)}) %collective-permute-start.1) | collective-permute-done | bytes 131104 | tf_op jit(solution)/shard_map/ppermute | solution.py:69
  19.1 2.8 %collective-permute-done.4.b3 = bf16[64,1024]{1,0:T(8,128)(2,1)S(1)} collective-permute-done((bf16[64,1024]{1,0:T(8,128)(2,1)S(1)}, bf16[64,1024]{1,0:T(8,128)(2,1)S(1)}, u32[]{:S(2)}, u32[]{:S(2)}) %collective-permute-start.4) | collective-permute-done | bytes 131104 | tf_op jit(solution)/shard_map/ppermute | solution.py:69
  21.9 4.3 %shard_map.52 = (f32[256,4992]{1,0:T(8,128)S(1)}, bf16[1664,1024]{1,0:T(8,128)(2,1)S(1)}, bf16[1664,1024]{1,0:T(8,128)(2,1)S(1)}) custom-call(s32[4]{0:T(128)S(1)} %pad_add_fusion.at, bf16[64,2048]{1,0:T(8,128)(2,1)S(1)} %copy-done.2, bf16[64,2048]{1,0:T(8,128)(2,1)S(1)} %collective-permute-done.b1.refs_9_, bf16[64,1024]{1,0:T(8,128)(2,1)S(1)} %collective-permute-done.3.b2, ...), custom_call_target="tpu_custom_call" | custom-call | flops 2617245696 | bytes 6815744 | tf_op jit(solution)/shard_map/pallas_call | solution.py:130
  26.3 3.7 %shard_map.55 = (f32[128,1664]{1,0:T(8,128)S(1)}, f32[128,1664]{1,0:T(8,128)S(1)}, bf16[1664,1024]{1,0:T(8,128)(2,1)S(1)}) custom-call(s32[4]{0:T(128)S(1)} %pad_add_fusion.at, bf16[64,2048]{1,0:T(8,128)(2,1)S(1)} %copy-done.2, bf16[64,2048]{1,0:T(8,128)(2,1)S(1)} %collective-permute-done.b1.refs_9_, bf16[64,1024]{1,0:T(8,128)(2,1)S(1)} %collective-permute-done.1.b2, ...), custom_call_target="tpu_custom_call" | custom-call | flops 872415232 | bytes 3407872 | tf_op jit(solution)/shard_map/pallas_call | solution.py:184
  31.0 2.5 %shard_map.54 = (f32[128,1664]{1,0:T(8,128)S(1)}, f32[128,1664]{1,0:T(8,128)S(1)}, bf16[1664,1024]{1,0:T(8,128)(2,1)S(1)}) custom-call(s32[4]{0:T(128)S(1)} %pad_add_fusion.at, bf16[64,2048]{1,0:T(8,128)(2,1)S(1)} %copy-done.2, bf16[64,2048]{1,0:T(8,128)(2,1)S(1)} %collective-permute-done.b1.refs_9_, bf16[64,1024]{1,0:T(8,128)(2,1)S(1)} %collective-permute-done.1.b2, ...), custom_call_target="tpu_custom_call" | custom-call | flops 872415232 | bytes 3407872 | tf_op jit(solution)/shard_map/pallas_call | solution.py:184
  34.5 3.6 %shard_map.56 = (f32[128,1664]{1,0:T(8,128)S(1)}, f32[128,1664]{1,0:T(8,128)}) custom-call(s32[4]{0:T(128)S(1)} %pad_add_fusion.at, bf16[64,2048]{1,0:T(8,128)(2,1)S(1)} %copy-done.2, bf16[64,2048]{1,0:T(8,128)(2,1)S(1)} %collective-permute-done.b1.refs_9_, bf16[64,2048]{1,0:T(8,128)(2,1)S(1)} %constant_dynamic-update-slice_fusion.b2.refs_10_, ...), custom_call_target="tpu_custom_call" | custom-call | flops 1744830464 | bytes 6815744 | tf_op jit(solution)/shard_map/pallas_call | solution.py:184
  38.1 1.5 %collective-permute-start.20 = (bf16[64,2048]{1,0:T(8,128)(2,1)S(1)}, bf16[64,2048]{1,0:T(8,128)(2,1)}, u32[]{:S(2)}, u32[]{:S(2)}) collective-permute-start(bf16[64,2048]{1,0:T(8,128)(2,1)S(1)} %copy-done.2), channel_id=1, source_target_pairs={{0,16},{16,0},{1,17},{17,1},{2,18},{18,2},{3,19},{19,3},{4,20},{20... | collective-permute-start | bytes 786440 | tf_op jit(solution)/shard_map/ppermute | solution.py:69
  39.8 1.2 %constant_dynamic-slice_fusion = (bf16[64,3328]{1,0:T(8,128)(2,1)S(1)}, bf16[64,3328]{1,0:T(8,128)(2,1)S(1)}) fusion(bf16[64,6656]{1,0:T(8,128)(2,1)} %param.4, s32[]{:T(128)S(6)} %select_n.24, s32[]{:T(128)S(6)} %select_n.23), kind=kLoop, calls=%fused_computation.21 | loop fusion | bytes 1703944 | tf_op jit(solution)/shard_map/dynamic_slice | solution.py:296
  41.6 1.5 %collective-permute-start.13 = (bf16[64,3328]{1,0:T(8,128)(2,1)S(1)}, bf16[64,3328]{1,0:T(8,128)(2,1)S(1)}, u32[]{:S(2)}, u32[]{:S(2)}) collective-permute-start(bf16[64,3328]{1,0:T(8,128)(2,1)S(1)} %get-tuple-element.37.refs_0_), channel_id=1, source_target_pairs={{0,8},{4,12},{8,0},{12,4},{1,9},{5,13},{9,1},{13,5},{2,10},{6,14},... | collective-permute-start | bytes 1277960 | tf_op jit(solution)/shard_map/ppermute | solution.py:69
  43.1 2.4 %copy-done.1 = f32[256,4992]{1,0:T(8,128)S(1)} copy-done((f32[256,4992]{1,0:T(8,128)S(1)}, f32[256,4992]{1,0:T(8,128)}, u32[]{:S(2)}) %copy-start.1) | copy-done | bytes 5111832
  45.5 2.0 %copy-done.4 = bf16[1664,1024]{1,0:T(8,128)(2,1)S(1)} copy-done((bf16[1664,1024]{1,0:T(8,128)(2,1)S(1)}, bf16[1664,1024]{1,0:T(8,128)(2,1)}, u32[]{:S(2)}) %copy-start.4) | copy-done | bytes 3407896
  47.5 1.7 %shard_map.53 = (f32[128,1664]{1,0:T(8,128)S(1)}, f32[128,1664]{1,0:T(8,128)S(1)}) custom-call(s32[4]{0:T(128)S(1)} %pad_add_fusion.at, bf16[64,2048]{1,0:T(8,128)(2,1)S(1)} %copy-done.2, bf16[64,2048]{1,0:T(8,128)(2,1)S(1)} %collective-permute-done.b1.refs_9_, bf16[64,1024]{1,0:T(8,128)(2,1)S(1)} %collective-permute-done.1.b2, ...), custom_call_target="tpu_custom_call" | custom-call | flops 872415232 | bytes 3407872 | tf_op jit(solution)/shard_map/pallas_call | solution.py:184
  49.3 1.1 %fusion.3 = bf16[64,1664]{1,0:T(8,128)(2,1)S(1)} fusion(f32[128,1664]{1,0:T(8,128)} %collective-permute-done.11.refs_10_, f32[128,1664]{1,0:T(8,128)S(1)} %get-tuple-element.34.refs_9_), kind=kLoop, calls=%fused_computation.7 | loop fusion | flops 958464 | bytes 1064960 | tf_op jit(solution)/shard_map/convert_element_type | solution.py:56
  51.2 4.7 %collective-permute-done.16.refs_4_ = bf16[64,3328]{1,0:T(8,128)(2,1)S(1)} collective-permute-done((bf16[64,3328]{1,0:T(8,128)(2,1)S(1)}, bf16[64,3328]{1,0:T(8,128)(2,1)S(1)}, u32[]{:S(2)}, u32[]{:S(2)}) %collective-permute-start.16) | collective-permute-done | bytes 426016 | tf_op jit(solution)/shard_map/ppermute | solution.py:69
  55.9 1.5 %collective-permute-start.22 = (bf16[64,2048]{1,0:T(8,128)(2,1)S(1)}, bf16[64,2048]{1,0:T(8,128)(2,1)S(1)}, u32[]{:S(2)}, u32[]{:S(2)}) collective-permute-start(bf16[64,2048]{1,0:T(8,128)(2,1)S(1)} %copy-done.8), channel_id=1, source_target_pairs={{0,16},{16,0},{1,17},{17,1},{2,18},{18,2},{3,19},{19,3},{4,20},{20... | collective-permute-start | bytes 786440 | tf_op jit(solution)/shard_map/ppermute | solution.py:69
  57.4 1.5 %collective-permute-start.17 = (bf16[64,3328]{1,0:T(8,128)(2,1)S(1)}, bf16[64,3328]{1,0:T(8,128)(2,1)S(1)}, u32[]{:S(2)}, u32[]{:S(2)}) collective-permute-start(bf16[64,3328]{1,0:T(8,128)(2,1)S(1)} %collective-permute-done.16.refs_4_), channel_id=1, source_target_pairs={{0,8},{4,12},{8,0},{12,4},{1,9},{5,13},{9,1},{13,5},{2,10},{6,14},... | collective-permute-start | bytes 1277960 | tf_op jit(solution)/shard_map/ppermute | solution.py:69
  59.1 4.7 %collective-permute-done.22.refs_14_ = bf16[64,2048]{1,0:T(8,128)(2,1)S(1)} collective-permute-done((bf16[64,2048]{1,0:T(8,128)(2,1)S(1)}, bf16[64,2048]{1,0:T(8,128)(2,1)S(1)}, u32[]{:S(2)}, u32[]{:S(2)}) %collective-permute-start.22) | collective-permute-done | bytes 262176 | tf_op jit(solution)/shard_map/ppermute | solution.py:69
  63.8 1.5 %collective-permute-start.21 = (bf16[64,2048]{1,0:T(8,128)(2,1)S(1)}, bf16[64,2048]{1,0:T(8,128)(2,1)S(1)}, u32[]{:S(2)}, u32[]{:S(2)}) collective-permute-start(bf16[64,2048]{1,0:T(8,128)(2,1)S(1)} %collective-permute-done.b1.refs_9_), channel_id=1, source_target_pairs={{0,16},{16,0},{1,17},{17,1},{2,18},{18,2},{3,19},{19,3},{4,20},{20... | collective-permute-start | bytes 786440 | tf_op jit(solution)/shard_map/ppermute | solution.py:69
  65.3 2.4 %collective-permute-start.23 = (bf16[64,2048]{1,0:T(8,128)(2,1)S(1)}, bf16[64,2048]{1,0:T(8,128)(2,1)S(1)}, u32[]{:S(2)}, u32[]{:S(2)}) collective-permute-start(bf16[64,2048]{1,0:T(8,128)(2,1)S(1)} %collective-permute-done.22.refs_14_), channel_id=1, source_target_pairs={{0,1},{1,0},{2,3},{3,2},{4,5},{5,4},{6,7},{7,6},{8,9},{9,8},{10,11... | collective-permute-start | bytes 786440 | tf_op jit(solution)/shard_map/ppermute | solution.py:69
  69.2 1.6 %collective-permute-done.21.refs_13_ = bf16[64,2048]{1,0:T(8,128)(2,1)S(1)} collective-permute-done((bf16[64,2048]{1,0:T(8,128)(2,1)S(1)}, bf16[64,2048]{1,0:T(8,128)(2,1)S(1)}, u32[]{:S(2)}, u32[]{:S(2)}) %collective-permute-start.21) | collective-permute-done | bytes 262176 | tf_op jit(solution)/shard_map/ppermute | solution.py:69
  70.8 1.5 %collective-permute-start.12 = (bf16[64,1664]{1,0:T(8,128)(2,1)S(1)}, bf16[64,1664]{1,0:T(8,128)(2,1)S(1)}, u32[]{:S(2)}, u32[]{:S(2)}) collective-permute-start(bf16[64,1664]{1,0:T(8,128)(2,1)S(1)} %fusion.3), channel_id=1, source_target_pairs={{0,8},{4,12},{8,0},{12,4},{1,9},{5,13},{9,1},{13,5},{2,10},{6,14},... | collective-permute-start | bytes 638984 | tf_op jit(solution)/shard_map/ppermute | solution.py:69
  72.7 1.5 %collective-permute-start.10 = (bf16[64,1664]{1,0:T(8,128)(2,1)S(1)}, bf16[64,1664]{1,0:T(8,128)(2,1)S(1)}, u32[]{:S(2)}, u32[]{:S(2)}) collective-permute-start(bf16[64,1664]{1,0:T(8,128)(2,1)S(1)} %fusion.2), channel_id=1, source_target_pairs={{0,8},{4,12},{8,0},{12,4},{1,9},{5,13},{9,1},{13,5},{2,10},{6,14},... | collective-permute-start | bytes 638984 | tf_op jit(solution)/shard_map/ppermute | solution.py:69
  74.7 1.5 %collective-permute-start.6 = (bf16[64,1664]{1,0:T(8,128)(2,1)S(1)}, bf16[64,1664]{1,0:T(8,128)(2,1)S(1)}, u32[]{:S(2)}, u32[]{:S(2)}) collective-permute-start(bf16[64,1664]{1,0:T(8,128)(2,1)S(1)} %fusion), channel_id=1, source_target_pairs={{0,8},{4,12},{8,0},{12,4},{1,9},{5,13},{9,1},{13,5},{2,10},{6,14},... | collective-permute-start | bytes 638984 | tf_op jit(solution)/shard_map/ppermute | solution.py:69
  76.2 11.4 %shard_map.58 = bf16[3328,2048]{1,0:T(8,128)(2,1)} custom-call(s32[4]{0:T(128)S(1)} %pad_add_fusion.at, bf16[64,3328]{1,0:T(8,128)(2,1)S(1)} %get-tuple-element.37.refs_0_, bf16[64,3328]{1,0:T(8,128)(2,1)S(1)} %collective-permute-done.13.refs_1_, bf16[64,3328]{1,0:T(8,128)(2,1)S(1)} %collective-permute-done.14.refs_2_, ...), custom_call_target="tpu_custom_call" | custom-call | flops 6979321856 | bytes 13631488 | tf_op jit(solution)/shard_map/pallas_call | solution.py:272
  87.8 2.3 %collective-permute-done.6.refs_2_ = bf16[64,1664]{1,0:T(8,128)(2,1)S(1)} collective-permute-done((bf16[64,1664]{1,0:T(8,128)(2,1)S(1)}, bf16[64,1664]{1,0:T(8,128)(2,1)S(1)}, u32[]{:S(2)}, u32[]{:S(2)}) %collective-permute-start.6) | collective-permute-done | bytes 213024 | tf_op jit(solution)/shard_map/ppermute | solution.py:69
  90.1 2.9 %shard_map.57 = bf16[64,6656]{1,0:T(8,128)(2,1)} custom-call(f32[128,1664]{1,0:T(8,128)S(1)} %get-tuple-element.24.refs_0_, f32[128,1664]{1,0:T(8,128)S(1)} %collective-permute-done.5.refs_1_, bf16[64,1664]{1,0:T(8,128)(2,1)S(1)} %collective-permute-done.6.refs_2_, f32[128,1664]{1,0:T(8,128)S(1)} %get-tuple-element.27.refs_3_, ...), custom_call_target="tpu_custom_call" | custom-call | flops 8519680 | bytes 5963776 | tf_op jit(solution)/shard_map/pallas_call | solution.py:227
  (60 shorter events, 7.2 us)
Async XLA Ops:
  1.6 14.0 %collective-permute-start.3 = (bf16[64,1024]{1,0:T(8,128)(2,1)S(1)}, bf16[64,1024]{1,0:T(8,128)(2,1)S(1)}, u32[]{:S(2)}, u32[]{:S(2)}) collective-permute-start(bf16[64,1024]{1,0:T(8,128)(2,1)S(1)} %get-tuple-element.38), channel_id=1, source_target_pairs={{0,3},{1,2},{2,1},{3,0},{4,7},{5,6},{6,5},{7,4},{8,11},{9,10},{10,... | collective-permute-start | bytes 393224 | tf_op jit(solution)/shard_map/ppermute | solution.py:69
  6.8 12.3 %collective-permute-start = (bf16[64,2048]{1,0:T(8,128)(2,1)}, bf16[64,2048]{1,0:T(8,128)(2,1)S(1)}, u32[]{:S(2)}, u32[]{:S(2)}) collective-permute-start(bf16[64,2048]{1,0:T(8,128)(2,1)} %refs_8_.1), channel_id=1, source_target_pairs={{0,1},{1,0},{2,3},{3,2},{4,5},{5,4},{6,7},{7,6},{8,9},{9,8},{10,11... | collective-permute-start | bytes 786440 | tf_op jit(solution)/shard_map/ppermute | solution.py:69
  6.8 12.3 %collective-permute-start.1 = (bf16[64,1024]{1,0:T(8,128)(2,1)S(1)}, bf16[64,1024]{1,0:T(8,128)(2,1)S(1)}, u32[]{:S(2)}, u32[]{:S(2)}) collective-permute-start(bf16[64,1024]{1,0:T(8,128)(2,1)S(1)} %get-tuple-element.39), channel_id=1, source_target_pairs={{0,3},{1,2},{2,1},{3,0},{4,7},{5,6},{6,5},{7,4},{8,11},{9,10},{10,... | collective-permute-start | bytes 393224 | tf_op jit(solution)/shard_map/ppermute | solution.py:69
  10.8 11.2 %copy-start.2 = (bf16[64,2048]{1,0:T(8,128)(2,1)S(1)}, bf16[64,2048]{1,0:T(8,128)(2,1)}, u32[]{:S(2)}) copy-start(bf16[64,2048]{1,0:T(8,128)(2,1)} %refs_8_.1) | copy-start | bytes 786436
  15.6 6.4 %collective-permute-start.4 = (bf16[64,1024]{1,0:T(8,128)(2,1)S(1)}, bf16[64,1024]{1,0:T(8,128)(2,1)S(1)}, u32[]{:S(2)}, u32[]{:S(2)}) collective-permute-start(bf16[64,1024]{1,0:T(8,128)(2,1)S(1)} %collective-permute-done.3.b2), channel_id=1, source_target_pairs={{0,1},{1,0},{2,3},{3,2},{4,5},{5,4},{6,7},{7,6},{8,9},{9,8},{10,11... | collective-permute-start | bytes 393224 | tf_op jit(solution)/shard_map/ppermute | solution.py:69
  19.1 7.2 %collective-permute-start.2 = (bf16[64,1024]{1,0:T(8,128)(2,1)S(1)}, bf16[64,1024]{1,0:T(8,128)(2,1)S(1)}, u32[]{:S(2)}, u32[]{:S(2)}) collective-permute-start(bf16[64,1024]{1,0:T(8,128)(2,1)S(1)} %collective-permute-done.1.b2), channel_id=1, source_target_pairs={{0,1},{1,0},{2,3},{3,2},{4,5},{5,4},{6,7},{7,6},{8,9},{9,8},{10,11... | collective-permute-start | bytes 393224 | tf_op jit(solution)/shard_map/ppermute | solution.py:69
  19.1 15.4 %copy-start.7 = (bf16[64,2048]{1,0:T(8,128)(2,1)}, bf16[64,2048]{1,0:T(8,128)(2,1)S(1)}, u32[]{:S(2)}) copy-start(bf16[64,2048]{1,0:T(8,128)(2,1)S(1)} %constant_dynamic-update-slice_fusion.b2.refs_10_) | copy-start | bytes 786436
  26.3 4.7 %copy-start = (f32[256,4992]{1,0:T(8,128)}, f32[256,4992]{1,0:T(8,128)S(1)}, u32[]{:S(2)}) copy-start(f32[256,4992]{1,0:T(8,128)S(1)} %get-tuple-element.23.refs_1_) | copy-start | bytes 15335428
  34.5 3.6 %copy-start.5 = (bf16[64,2048]{1,0:T(8,128)(2,1)}, bf16[64,2048]{1,0:T(8,128)(2,1)S(1)}, u32[]{:S(2)}) copy-start(bf16[64,2048]{1,0:T(8,128)(2,1)S(1)} %constant_dynamic-update-slice_fusion.2.b3.refs_11_) | copy-start | bytes 786436
  38.1 11.1 %collective-permute-start.11 = (f32[128,1664]{1,0:T(8,128)}, f32[128,1664]{1,0:T(8,128)}, u32[]{:S(2)}, u32[]{:S(2)}) collective-permute-start(f32[128,1664]{1,0:T(8,128)} %get-tuple-element.35), channel_id=1, source_target_pairs={{0,4},{4,0},{8,12},{12,8},{1,5},{5,1},{9,13},{13,9},{2,6},{6,2},{1... | collective-permute-start | bytes 2555912 | tf_op jit(solution)/shard_map/ppermute | solution.py:69
  38.1 13.1 %collective-permute-start.20 = (bf16[64,2048]{1,0:T(8,128)(2,1)S(1)}, bf16[64,2048]{1,0:T(8,128)(2,1)}, u32[]{:S(2)}, u32[]{:S(2)}) collective-permute-start(bf16[64,2048]{1,0:T(8,128)(2,1)S(1)} %copy-done.2), channel_id=1, source_target_pairs={{0,16},{16,0},{1,17},{17,1},{2,18},{18,2},{3,19},{19,3},{4,20},{20... | collective-permute-start | bytes 786440 | tf_op jit(solution)/shard_map/ppermute | solution.py:69
  39.6 10.9 %collective-permute-start.9 = (f32[128,1664]{1,0:T(8,128)}, f32[128,1664]{1,0:T(8,128)S(1)}, u32[]{:S(2)}, u32[]{:S(2)}) collective-permute-start(f32[128,1664]{1,0:T(8,128)} %copy-done.11), channel_id=1, source_target_pairs={{0,4},{4,0},{8,12},{12,8},{1,5},{5,1},{9,13},{13,9},{2,6},{6,2},{1... | collective-permute-start | bytes 2555912 | tf_op jit(solution)/shard_map/ppermute | solution.py:69
  41.0 14.9 %collective-permute-start.16 = (bf16[64,3328]{1,0:T(8,128)(2,1)S(1)}, bf16[64,3328]{1,0:T(8,128)(2,1)S(1)}, u32[]{:S(2)}, u32[]{:S(2)}) collective-permute-start(bf16[64,3328]{1,0:T(8,128)(2,1)S(1)} %get-tuple-element.36), channel_id=1, source_target_pairs={{0,16},{16,0},{1,17},{17,1},{2,18},{18,2},{3,19},{19,3},{4,20},{20... | collective-permute-start | bytes 1277960 | tf_op jit(solution)/shard_map/ppermute | solution.py:69
  41.6 23.7 %collective-permute-start.13 = (bf16[64,3328]{1,0:T(8,128)(2,1)S(1)}, bf16[64,3328]{1,0:T(8,128)(2,1)S(1)}, u32[]{:S(2)}, u32[]{:S(2)}) collective-permute-start(bf16[64,3328]{1,0:T(8,128)(2,1)S(1)} %get-tuple-element.37.refs_0_), channel_id=1, source_target_pairs={{0,8},{4,12},{8,0},{12,4},{1,9},{5,13},{9,1},{13,5},{2,10},{6,14},... | collective-permute-start | bytes 1277960 | tf_op jit(solution)/shard_map/ppermute | solution.py:69
  43.1 2.4 %copy-start.1 = (f32[256,4992]{1,0:T(8,128)S(1)}, f32[256,4992]{1,0:T(8,128)}, u32[]{:S(2)}) copy-start(f32[256,4992]{1,0:T(8,128)} %copy-done) | copy-start | bytes 15335428
  45.5 2.0 %copy-start.4 = (bf16[1664,1024]{1,0:T(8,128)(2,1)S(1)}, bf16[1664,1024]{1,0:T(8,128)(2,1)}, u32[]{:S(2)}) copy-start(bf16[1664,1024]{1,0:T(8,128)(2,1)} %copy-done.3) | copy-start | bytes 10223620
  47.5 8.4 %copy-start.8 = (bf16[64,2048]{1,0:T(8,128)(2,1)S(1)}, bf16[64,2048]{1,0:T(8,128)(2,1)}, u32[]{:S(2)}) copy-start(bf16[64,2048]{1,0:T(8,128)(2,1)} %copy-done.7) | copy-start | bytes 786436
  49.2 27.1 %copy-start.6 = (bf16[64,2048]{1,0:T(8,128)(2,1)S(1)}, bf16[64,2048]{1,0:T(8,128)(2,1)}, u32[]{:S(2)}) copy-start(bf16[64,2048]{1,0:T(8,128)(2,1)} %copy-done.5) | copy-start | bytes 786436
  49.2 8.2 %collective-permute-start.7 = (f32[128,1664]{1,0:T(8,128)S(1)}, f32[128,1664]{1,0:T(8,128)S(1)}, u32[]{:S(2)}, u32[]{:S(2)}) collective-permute-start(f32[128,1664]{1,0:T(8,128)S(1)} %copy-done.10), channel_id=1, source_target_pairs={{0,4},{4,0},{8,12},{12,8},{1,5},{5,1},{9,13},{13,9},{2,6},{6,2},{1... | collective-permute-start | bytes 2555912 | tf_op jit(solution)/shard_map/ppermute | solution.py:69
  50.5 18.1 %collective-permute-start.5 = (f32[128,1664]{1,0:T(8,128)S(1)}, f32[128,1664]{1,0:T(8,128)S(1)}, u32[]{:S(2)}, u32[]{:S(2)}) collective-permute-start(f32[128,1664]{1,0:T(8,128)S(1)} %get-tuple-element.25), channel_id=1, source_target_pairs={{0,4},{4,0},{8,12},{12,8},{1,5},{5,1},{9,13},{13,9},{2,6},{6,2},{1... | collective-permute-start | bytes 2555912 | tf_op jit(solution)/shard_map/ppermute | solution.py:69
  51.2 16.6 %collective-permute-start.14 = (bf16[64,3328]{1,0:T(8,128)(2,1)S(1)}, bf16[64,3328]{1,0:T(8,128)(2,1)S(1)}, u32[]{:S(2)}, u32[]{:S(2)}) collective-permute-start(bf16[64,3328]{1,0:T(8,128)(2,1)S(1)} %get-tuple-element.37.refs_0_), channel_id=1, source_target_pairs={{0,4},{4,0},{8,12},{12,8},{1,5},{5,1},{9,13},{13,9},{2,6},{6,2},{1... | collective-permute-start | bytes 1277960 | tf_op jit(solution)/shard_map/ppermute | solution.py:69
  55.9 7.9 %collective-permute-start.22 = (bf16[64,2048]{1,0:T(8,128)(2,1)S(1)}, bf16[64,2048]{1,0:T(8,128)(2,1)S(1)}, u32[]{:S(2)}, u32[]{:S(2)}) collective-permute-start(bf16[64,2048]{1,0:T(8,128)(2,1)S(1)} %copy-done.8), channel_id=1, source_target_pairs={{0,16},{16,0},{1,17},{17,1},{2,18},{18,2},{3,19},{19,3},{4,20},{20... | collective-permute-start | bytes 786440 | tf_op jit(solution)/shard_map/ppermute | solution.py:69
  57.4 11.1 %collective-permute-start.17 = (bf16[64,3328]{1,0:T(8,128)(2,1)S(1)}, bf16[64,3328]{1,0:T(8,128)(2,1)S(1)}, u32[]{:S(2)}, u32[]{:S(2)}) collective-permute-start(bf16[64,3328]{1,0:T(8,128)(2,1)S(1)} %collective-permute-done.16.refs_4_), channel_id=1, source_target_pairs={{0,8},{4,12},{8,0},{12,4},{1,9},{5,13},{9,1},{13,5},{2,10},{6,14},... | collective-permute-start | bytes 1277960 | tf_op jit(solution)/shard_map/ppermute | solution.py:69
  63.8 7.0 %collective-permute-start.21 = (bf16[64,2048]{1,0:T(8,128)(2,1)S(1)}, bf16[64,2048]{1,0:T(8,128)(2,1)S(1)}, u32[]{:S(2)}, u32[]{:S(2)}) collective-permute-start(bf16[64,2048]{1,0:T(8,128)(2,1)S(1)} %collective-permute-done.b1.refs_9_), channel_id=1, source_target_pairs={{0,16},{16,0},{1,17},{17,1},{2,18},{18,2},{3,19},{19,3},{4,20},{20... | collective-permute-start | bytes 786440 | tf_op jit(solution)/shard_map/ppermute | solution.py:69
  65.3 7.4 %collective-permute-start.23 = (bf16[64,2048]{1,0:T(8,128)(2,1)S(1)}, bf16[64,2048]{1,0:T(8,128)(2,1)S(1)}, u32[]{:S(2)}, u32[]{:S(2)}) collective-permute-start(bf16[64,2048]{1,0:T(8,128)(2,1)S(1)} %collective-permute-done.22.refs_14_), channel_id=1, source_target_pairs={{0,1},{1,0},{2,3},{3,2},{4,5},{5,4},{6,7},{7,6},{8,9},{9,8},{10,11... | collective-permute-start | bytes 786440 | tf_op jit(solution)/shard_map/ppermute | solution.py:69
  67.7 7.0 %collective-permute-start.18 = (bf16[64,3328]{1,0:T(8,128)(2,1)S(1)}, bf16[64,3328]{1,0:T(8,128)(2,1)S(1)}, u32[]{:S(2)}, u32[]{:S(2)}) collective-permute-start(bf16[64,3328]{1,0:T(8,128)(2,1)S(1)} %collective-permute-done.16.refs_4_), channel_id=1, source_target_pairs={{0,4},{4,0},{8,12},{12,8},{1,5},{5,1},{9,13},{13,9},{2,6},{6,2},{1... | collective-permute-start | bytes 1277960 | tf_op jit(solution)/shard_map/ppermute | solution.py:69
  68.5 5.7 %collective-permute-start.15 = (bf16[64,3328]{1,0:T(8,128)(2,1)S(1)}, bf16[64,3328]{1,0:T(8,128)(2,1)S(1)}, u32[]{:S(2)}, u32[]{:S(2)}) collective-permute-start(bf16[64,3328]{1,0:T(8,128)(2,1)S(1)} %collective-permute-done.13.refs_1_), channel_id=1, source_target_pairs={{0,4},{4,0},{8,12},{12,8},{1,5},{5,1},{9,13},{13,9},{2,6},{6,2},{1... | collective-permute-start | bytes 1277960 | tf_op jit(solution)/shard_map/ppermute | solution.py:69
  68.5 7.7 %collective-permute-start.19 = (bf16[64,3328]{1,0:T(8,128)(2,1)S(1)}, bf16[64,3328]{1,0:T(8,128)(2,1)S(1)}, u32[]{:S(2)}, u32[]{:S(2)}) collective-permute-start(bf16[64,3328]{1,0:T(8,128)(2,1)S(1)} %collective-permute-done.17.refs_5_), channel_id=1, source_target_pairs={{0,4},{4,0},{8,12},{12,8},{1,5},{5,1},{9,13},{13,9},{2,6},{6,2},{1... | collective-permute-start | bytes 1277960 | tf_op jit(solution)/shard_map/ppermute | solution.py:69
  70.8 16.9 %collective-permute-start.12 = (bf16[64,1664]{1,0:T(8,128)(2,1)S(1)}, bf16[64,1664]{1,0:T(8,128)(2,1)S(1)}, u32[]{:S(2)}, u32[]{:S(2)}) collective-permute-start(bf16[64,1664]{1,0:T(8,128)(2,1)S(1)} %fusion.3), channel_id=1, source_target_pairs={{0,8},{4,12},{8,0},{12,4},{1,9},{5,13},{9,1},{13,5},{2,10},{6,14},... | collective-permute-start | bytes 638984 | tf_op jit(solution)/shard_map/ppermute | solution.py:69
  72.7 14.9 %collective-permute-start.10 = (bf16[64,1664]{1,0:T(8,128)(2,1)S(1)}, bf16[64,1664]{1,0:T(8,128)(2,1)S(1)}, u32[]{:S(2)}, u32[]{:S(2)}) collective-permute-start(bf16[64,1664]{1,0:T(8,128)(2,1)S(1)} %fusion.2), channel_id=1, source_target_pairs={{0,8},{4,12},{8,0},{12,4},{1,9},{5,13},{9,1},{13,5},{2,10},{6,14},... | collective-permute-start | bytes 638984 | tf_op jit(solution)/shard_map/ppermute | solution.py:69
  74.2 13.6 %collective-permute-start.8 = (bf16[64,1664]{1,0:T(8,128)(2,1)S(1)}, bf16[64,1664]{1,0:T(8,128)(2,1)S(1)}, u32[]{:S(2)}, u32[]{:S(2)}) collective-permute-start(bf16[64,1664]{1,0:T(8,128)(2,1)S(1)} %fusion.1), channel_id=1, source_target_pairs={{0,8},{4,12},{8,0},{12,4},{1,9},{5,13},{9,1},{13,5},{2,10},{6,14},... | collective-permute-start | bytes 638984 | tf_op jit(solution)/shard_map/ppermute | solution.py:69
  74.7 15.4 %collective-permute-start.6 = (bf16[64,1664]{1,0:T(8,128)(2,1)S(1)}, bf16[64,1664]{1,0:T(8,128)(2,1)S(1)}, u32[]{:S(2)}, u32[]{:S(2)}) collective-permute-start(bf16[64,1664]{1,0:T(8,128)(2,1)S(1)} %fusion), channel_id=1, source_target_pairs={{0,8},{4,12},{8,0},{12,4},{1,9},{5,13},{9,1},{13,5},{2,10},{6,14},... | collective-permute-start | bytes 638984 | tf_op jit(solution)/shard_map/ppermute | solution.py:69
  (4 other events, 5.3 us)
